TPU v7x, 256 devices: a whole 4x4x8 slice. The times are simulated.
256 devices in a mesh: gx: 16 (over z_lo, x), gy: 16 (over z_hi, y, core).
Axes of the slice: x: 4, y: 4, z: 8 (z_hi: 2, z_lo: 4; z = z_hi * 4 + z_lo), core: 2. Of those that a mesh axis runs over, the one named last changes fastest.
Arguments:
- maps: bfloat16 [16, 16, 2048, 2048], P('gx', 'gy'), may hold values from -0.125 to 0.125
- sources: float32 [16, 16, 256, 2048], P('gx', 'gy'), may hold values from -6 to 6
- traces: bfloat16 [16, 16, 256, 2048], P('gx', 'gy'), may hold values from -6 to 6
Outputs:
- outgoing: bfloat16 [16, 16, 256, 2048], P('gx', 'gy')
All inputs are finite; a program needn't handle non-finite values.
Results may differ from a plain program's by a relative error of at most 0.0085.
Values may be sent and summed in bfloat16 or wider, within the bound.
No kernel may reach another device: no remote copies, remote signals or barrier semaphores. Data moves between devices by JAX's collectives and lax.ppermute only.
A program may use at most 64 MiB of HBM per device.

v0:
```python
import jax
import jax.numpy as jnp
from jax import lax
from jax.sharding import PartitionSpec as P

TICKS = 8


def from_behind(array, axis, by):
    size = lax.axis_size(axis)
    pairs = [(i, i + by) for i in range(size) if 0 <= i + by < size]
    return lax.ppermute(array, axis, pairs)


def project(state, weights, source, low, width):
    value = jnp.dot(state, weights[:, low : low + width], preferred_element_type=jnp.float32)
    return (value + source[:, low : low + width]).astype(jnp.bfloat16)


def two_faces(state, weights, source, low, face):
    both = project(state, weights, source, low, 2 * face)
    return (both[:, :face], both[:, face:])


def downstream(state, weights, source, face):
    east, north = two_faces(state, weights, source, 2 * face, face)
    west_new = from_behind(east, "gx", 1)
    south_new = from_behind(north, "gy", 1)
    return jnp.concatenate([west_new, south_new, state[:, 2 * face :]], axis=1)


def upstream(state, weights, source, face):
    west, south = two_faces(state, weights, source, 0, face)
    east_new = from_behind(west, "gx", -1)
    north_new = from_behind(south, "gy", -1)
    return jnp.concatenate([state[:, : 2 * face], east_new, north_new], axis=1)


def advance(state, weights, source, face, going_down):
    if going_down:
        return downstream(state, weights, source, face)
    return upstream(state, weights, source, face)


def on_device(maps, sources, traces):
    weights = maps[0, 0]
    source = sources[0, 0]
    state = traces[0, 0]
    face = weights.shape[0] // 4
    rows = state.shape[0]
    for tick in range(TICKS - 1):
        going_down = tick < TICKS // 2
        half = rows // 2
        upper = advance(state[:half], weights, source[:half], face, going_down)
        lower = advance(state[half:], weights, source[half:], face, going_down)
        state = jnp.concatenate([upper, lower], axis=0)
    result = project(state, weights, source, 0, 4 * face)
    return result[None, None]


def solution(mesh):
    return jax.shard_map(
        on_device,
        mesh=mesh,
        in_specs=(P("gx", "gy", None, None), P("gx", "gy", None, None), P("gx", "gy", None, None)),
        out_specs=P("gx", "gy", None, None),
        check_vma=False,
    )
```

profile of v0, /device:TPU:61, one launch (start us, length us, event | category | flops | bytes accessed | tf_op | source)
XLA Modules:
  0.0 133.4 jit_solution(16536955813785226343)
XLA Ops:
  1.9 3.7 %fusion.50 = bf16[128,1024]{1,0:T(8,128)(2,1)S(1)} fusion(bf16[2048,2048]{1,0:T(8,128)(2,1)} %bitcast.17, f32[128,2048]{1,0:T(8,128)S(1)} %get-tuple-element.5, bf16[1,1,256,2048]{3,2,1,0:T(8,128)(2,1)S(1)} %copy-done.1), kind=kOutput, calls=%fused_computation.35 | convolution fusion | flops 537133056 | bytes 5505024 | tf_op jit(solution)/shard_map/dot_general | solution.py:16
  5.6 2.8 %collective-permute-start = (bf16[128,512]{1,0:T(8,128)(2,1)S(1)}, bf16[128,512]{1,0:T(8,128)(2,1)S(1)}, u32[]{:S(2)}, u32[]{:S(2)}) collective-permute-start(bf16[128,512]{1,0:T(8,128)(2,1)S(1)} %get-tuple-element.21), channel_id=1, source_target_pairs={{0,16},{16,32},{32,48},{48,64},{64,80},{80,96},{96,112},{112,128},... | collective-permute-start | bytes 393224 | tf_op jit(solution)/shard_map/ppermute | solution.py:12
  8.4 8.4 %collective-permute-start.1 = (bf16[128,512]{1,0:T(8,128)(2,1)S(1)}, bf16[128,512]{1,0:T(8,128)(2,1)S(1)}, u32[]{:S(2)}, u32[]{:S(2)}) collective-permute-start(bf16[128,512]{1,0:T(8,128)(2,1)S(1)} %get-tuple-element.22), channel_id=1, source_target_pairs={{0,1},{1,2},{2,3},{3,4},{4,5},{5,6},{6,7},{7,8},{8,9},{9,10},{10,1... | collective-permute-start | bytes 393224 | tf_op jit(solution)/shard_map/ppermute | solution.py:12
  17.7 2.6 %collective-permute-start.14 = (bf16[128,512]{1,0:T(8,128)(2,1)S(1)}, bf16[128,512]{1,0:T(8,128)(2,1)S(1)}, u32[]{:S(2)}, u32[]{:S(2)}) collective-permute-start(bf16[128,512]{1,0:T(8,128)(2,1)S(1)} %get-tuple-element.35), channel_id=1, source_target_pairs={{0,16},{16,32},{32,48},{48,64},{64,80},{80,96},{96,112},{112,128},... | collective-permute-start | bytes 393224 | tf_op jit(solution)/shard_map/ppermute | solution.py:12
  23.4 3.1 %collective-permute-start.2 = (bf16[128,512]{1,0:T(8,128)(2,1)S(1)}, bf16[128,512]{1,0:T(8,128)(2,1)S(1)}, u32[]{:S(2)}, u32[]{:S(2)}) collective-permute-start(bf16[128,512]{1,0:T(8,128)(2,1)S(1)} %get-tuple-element.19), channel_id=1, source_target_pairs={{0,16},{16,32},{32,48},{48,64},{64,80},{80,96},{96,112},{112,128},... | collective-permute-start | bytes 393224 | tf_op jit(solution)/shard_map/ppermute | solution.py:12
  26.5 7.0 %collective-permute-start.3 = (bf16[128,512]{1,0:T(8,128)(2,1)S(1)}, bf16[128,512]{1,0:T(8,128)(2,1)S(1)}, u32[]{:S(2)}, u32[]{:S(2)}) collective-permute-start(bf16[128,512]{1,0:T(8,128)(2,1)S(1)} %get-tuple-element.20), channel_id=1, source_target_pairs={{0,1},{1,2},{2,3},{3,4},{4,5},{5,6},{6,7},{7,8},{8,9},{9,10},{10,1... | collective-permute-start | bytes 393224 | tf_op jit(solution)/shard_map/ppermute | solution.py:12
  34.4 3.8 %collective-permute-start.16 = (bf16[128,512]{1,0:T(8,128)(2,1)S(1)}, bf16[128,512]{1,0:T(8,128)(2,1)S(1)}, u32[]{:S(2)}, u32[]{:S(2)}) collective-permute-start(bf16[128,512]{1,0:T(8,128)(2,1)S(1)} %get-tuple-element.33), channel_id=1, source_target_pairs={{0,16},{16,32},{32,48},{48,64},{64,80},{80,96},{96,112},{112,128},... | collective-permute-start | bytes 393224 | tf_op jit(solution)/shard_map/ppermute | solution.py:12
  41.2 3.1 %collective-permute-start.4 = (bf16[128,512]{1,0:T(8,128)(2,1)S(1)}, bf16[128,512]{1,0:T(8,128)(2,1)S(1)}, u32[]{:S(2)}, u32[]{:S(2)}) collective-permute-start(bf16[128,512]{1,0:T(8,128)(2,1)S(1)} %get-tuple-element.17), channel_id=1, source_target_pairs={{0,16},{16,32},{32,48},{48,64},{64,80},{80,96},{96,112},{112,128},... | collective-permute-start | bytes 393224 | tf_op jit(solution)/shard_map/ppermute | solution.py:12
  44.4 7.8 %collective-permute-start.5 = (bf16[128,512]{1,0:T(8,128)(2,1)S(1)}, bf16[128,512]{1,0:T(8,128)(2,1)S(1)}, u32[]{:S(2)}, u32[]{:S(2)}) collective-permute-start(bf16[128,512]{1,0:T(8,128)(2,1)S(1)} %get-tuple-element.18), channel_id=1, source_target_pairs={{0,1},{1,2},{2,3},{3,4},{4,5},{5,6},{6,7},{7,8},{8,9},{9,10},{10,1... | collective-permute-start | bytes 393224 | tf_op jit(solution)/shard_map/ppermute | solution.py:12
  53.0 2.7 %collective-permute-start.18 = (bf16[128,512]{1,0:T(8,128)(2,1)S(1)}, bf16[128,512]{1,0:T(8,128)(2,1)S(1)}, u32[]{:S(2)}, u32[]{:S(2)}) collective-permute-start(bf16[128,512]{1,0:T(8,128)(2,1)S(1)} %get-tuple-element.31), channel_id=1, source_target_pairs={{0,16},{16,32},{32,48},{48,64},{64,80},{80,96},{96,112},{112,128},... | collective-permute-start | bytes 393224 | tf_op jit(solution)/shard_map/ppermute | solution.py:12
  58.7 2.8 %collective-permute-start.6 = (bf16[128,512]{1,0:T(8,128)(2,1)S(1)}, bf16[128,512]{1,0:T(8,128)(2,1)S(1)}, u32[]{:S(2)}, u32[]{:S(2)}) collective-permute-start(bf16[128,512]{1,0:T(8,128)(2,1)S(1)} %get-tuple-element.15), channel_id=1, source_target_pairs={{0,16},{16,32},{32,48},{48,64},{64,80},{80,96},{96,112},{112,128},... | collective-permute-start | bytes 393224 | tf_op jit(solution)/shard_map/ppermute | solution.py:12
  61.6 7.0 %collective-permute-start.7 = (bf16[128,512]{1,0:T(8,128)(2,1)S(1)}, bf16[128,512]{1,0:T(8,128)(2,1)S(1)}, u32[]{:S(2)}, u32[]{:S(2)}) collective-permute-start(bf16[128,512]{1,0:T(8,128)(2,1)S(1)} %get-tuple-element.16), channel_id=1, source_target_pairs={{0,1},{1,2},{2,3},{3,4},{4,5},{5,6},{6,7},{7,8},{8,9},{9,10},{10,1... | collective-permute-start | bytes 393224 | tf_op jit(solution)/shard_map/ppermute | solution.py:12
  69.4 2.6 %collective-permute-start.20 = (bf16[128,512]{1,0:T(8,128)(2,1)S(1)}, bf16[128,512]{1,0:T(8,128)(2,1)S(1)}, u32[]{:S(2)}, u32[]{:S(2)}) collective-permute-start(bf16[128,512]{1,0:T(8,128)(2,1)S(1)} %get-tuple-element.29), channel_id=1, source_target_pairs={{0,16},{16,32},{32,48},{48,64},{64,80},{80,96},{96,112},{112,128},... | collective-permute-start | bytes 393224 | tf_op jit(solution)/shard_map/ppermute | solution.py:12
  75.1 2.7 %collective-permute-start.8 = (bf16[128,512]{1,0:T(8,128)(2,1)S(1)}, bf16[128,512]{1,0:T(8,128)(2,1)S(1)}, u32[]{:S(2)}, u32[]{:S(2)}) collective-permute-start(bf16[128,512]{1,0:T(8,128)(2,1)S(1)} %get-tuple-element.13), channel_id=1, source_target_pairs={{16,0},{32,16},{48,32},{64,48},{80,64},{96,80},{112,96},{128,112},... | collective-permute-start | bytes 393224 | tf_op jit(solution)/shard_map/ppermute | solution.py:12
  77.8 2.7 %collective-permute-start.9 = (bf16[128,512]{1,0:T(8,128)(2,1)S(1)}, bf16[128,512]{1,0:T(8,128)(2,1)S(1)}, u32[]{:S(2)}, u32[]{:S(2)}) collective-permute-start(bf16[128,512]{1,0:T(8,128)(2,1)S(1)} %get-tuple-element.14), channel_id=1, source_target_pairs={{1,0},{2,1},{3,2},{4,3},{5,4},{6,5},{7,6},{8,7},{9,8},{10,9},{11,1... | collective-permute-start | bytes 393224 | tf_op jit(solution)/shard_map/ppermute | solution.py:12
  81.3 3.4 %collective-permute-start.22 = (bf16[128,512]{1,0:T(8,128)(2,1)S(1)}, bf16[128,512]{1,0:T(8,128)(2,1)S(1)}, u32[]{:S(2)}, u32[]{:S(2)}) collective-permute-start(bf16[128,512]{1,0:T(8,128)(2,1)S(1)} %get-tuple-element.27), channel_id=1, source_target_pairs={{16,0},{32,16},{48,32},{64,48},{80,64},{96,80},{112,96},{128,112},... | collective-permute-start | bytes 393224 | tf_op jit(solution)/shard_map/ppermute | solution.py:12
  86.9 3.2 %collective-permute-done.9 = bf16[128,512]{1,0:T(8,128)(2,1)S(1)} collective-permute-done((bf16[128,512]{1,0:T(8,128)(2,1)S(1)}, bf16[128,512]{1,0:T(8,128)(2,1)S(1)}, u32[]{:S(2)}, u32[]{:S(2)}) %collective-permute-start.9) | collective-permute-done | bytes 131104 | tf_op jit(solution)/shard_map/ppermute | solution.py:12
  90.9 3.6 %collective-permute-start.10 = (bf16[128,512]{1,0:T(8,128)(2,1)S(1)}, bf16[128,512]{1,0:T(8,128)(2,1)S(1)}, u32[]{:S(2)}, u32[]{:S(2)}) collective-permute-start(bf16[128,512]{1,0:T(8,128)(2,1)S(1)} %get-tuple-element.11), channel_id=1, source_target_pairs={{16,0},{32,16},{48,32},{64,48},{80,64},{96,80},{112,96},{128,112},... | collective-permute-start | bytes 393224 | tf_op jit(solution)/shard_map/ppermute | solution.py:12
  97.8 2.3 %collective-permute-start.24 = (bf16[128,512]{1,0:T(8,128)(2,1)S(1)}, bf16[128,512]{1,0:T(8,128)(2,1)S(1)}, u32[]{:S(2)}, u32[]{:S(2)}) collective-permute-start(bf16[128,512]{1,0:T(8,128)(2,1)S(1)} %get-tuple-element.25), channel_id=1, source_target_pairs={{16,0},{32,16},{48,32},{64,48},{80,64},{96,80},{112,96},{128,112},... | collective-permute-start | bytes 393224 | tf_op jit(solution)/shard_map/ppermute | solution.py:12
  102.0 4.8 %collective-permute-done.11 = bf16[128,512]{1,0:T(8,128)(2,1)S(1)} collective-permute-done((bf16[128,512]{1,0:T(8,128)(2,1)S(1)}, bf16[128,512]{1,0:T(8,128)(2,1)S(1)}, u32[]{:S(2)}, u32[]{:S(2)}) %collective-permute-start.11) | collective-permute-done | bytes 131104 | tf_op jit(solution)/shard_map/ppermute | solution.py:12
  113.2 4.6 %collective-permute-start.26 = (bf16[128,512]{1,0:T(8,128)(2,1)S(1)}, bf16[128,512]{1,0:T(8,128)(2,1)S(1)}, u32[]{:S(2)}, u32[]{:S(2)}) collective-permute-start(bf16[128,512]{1,0:T(8,128)(2,1)S(1)} %get-tuple-element.23), channel_id=1, source_target_pairs={{16,0},{32,16},{48,32},{64,48},{80,64},{96,80},{112,96},{128,112},... | collective-permute-start | bytes 393224 | tf_op jit(solution)/shard_map/ppermute | solution.py:12
  119.7 2.5 %collective-permute-done.13 = bf16[128,512]{1,0:T(8,128)(2,1)S(1)} collective-permute-done((bf16[128,512]{1,0:T(8,128)(2,1)S(1)}, bf16[128,512]{1,0:T(8,128)(2,1)S(1)}, u32[]{:S(2)}, u32[]{:S(2)}) %collective-permute-start.13) | collective-permute-done | bytes 131104 | tf_op jit(solution)/shard_map/ppermute | solution.py:12
  122.2 7.8 %collective-permute-done.27 = bf16[128,512]{1,0:T(8,128)(2,1)S(1)} collective-permute-done((bf16[128,512]{1,0:T(8,128)(2,1)S(1)}, bf16[128,512]{1,0:T(8,128)(2,1)S(1)}, u32[]{:S(2)}, u32[]{:S(2)}) %collective-permute-start.27) | collective-permute-done | bytes 131104 | tf_op jit(solution)/shard_map/ppermute | solution.py:12
  130.1 3.3 %fusion.1 = bf16[1,1,256,2048]{3,2,1,0:T(8,128)(2,1)} fusion(f32[1,1,256,2048]{3,2,1,0:T(8,128)S(1)} %copy-done, bf16[128,512]{1,0:T(8,128)(2,1)S(1)} %collective-permute-done.27, bf16[128,512]{1,0:T(8,128)(2,1)S(1)} %collective-permute-done.26, bf16[128,512]{1,0:T(8,128)(2,1)S(1)} %collective-permute-done.21, ...), kind=kOutput, calls=%fused_computation.2 | convolution fusion | flops 2156920832 | bytes 12582912 | tf_op jit(solution)/shard_map/dot_general | solution.py:16
  (71 shorter events, 34.3 us)
Async XLA Ops:
  5.6 17.0 %collective-permute-start = (bf16[128,512]{1,0:T(8,128)(2,1)S(1)}, bf16[128,512]{1,0:T(8,128)(2,1)S(1)}, u32[]{:S(2)}, u32[]{:S(2)}) collective-permute-start(bf16[128,512]{1,0:T(8,128)(2,1)S(1)} %get-tuple-element.21), channel_id=1, source_target_pairs={{0,16},{16,32},{32,48},{48,64},{64,80},{80,96},{96,112},{112,128},... | collective-permute-start | bytes 393224 | tf_op jit(solution)/shard_map/ppermute | solution.py:12
  8.4 14.2 %collective-permute-start.1 = (bf16[128,512]{1,0:T(8,128)(2,1)S(1)}, bf16[128,512]{1,0:T(8,128)(2,1)S(1)}, u32[]{:S(2)}, u32[]{:S(2)}) collective-permute-start(bf16[128,512]{1,0:T(8,128)(2,1)S(1)} %get-tuple-element.22), channel_id=1, source_target_pairs={{0,1},{1,2},{2,3},{3,4},{4,5},{5,6},{6,7},{7,8},{8,9},{9,10},{10,1... | collective-permute-start | bytes 393224 | tf_op jit(solution)/shard_map/ppermute | solution.py:12
  17.7 15.9 %collective-permute-start.14 = (bf16[128,512]{1,0:T(8,128)(2,1)S(1)}, bf16[128,512]{1,0:T(8,128)(2,1)S(1)}, u32[]{:S(2)}, u32[]{:S(2)}) collective-permute-start(bf16[128,512]{1,0:T(8,128)(2,1)S(1)} %get-tuple-element.35), channel_id=1, source_target_pairs={{0,16},{16,32},{32,48},{48,64},{64,80},{80,96},{96,112},{112,128},... | collective-permute-start | bytes 393224 | tf_op jit(solution)/shard_map/ppermute | solution.py:12
  20.2 13.4 %collective-permute-start.15 = (bf16[128,512]{1,0:T(8,128)(2,1)S(1)}, bf16[128,512]{1,0:T(8,128)(2,1)S(1)}, u32[]{:S(2)}, u32[]{:S(2)}) collective-permute-start(bf16[128,512]{1,0:T(8,128)(2,1)S(1)} %get-tuple-element.36), channel_id=1, source_target_pairs={{0,1},{1,2},{2,3},{3,4},{4,5},{5,6},{6,7},{7,8},{8,9},{9,10},{10,1... | collective-permute-start | bytes 393224 | tf_op jit(solution)/shard_map/ppermute | solution.py:12
  23.4 17.0 %collective-permute-start.2 = (bf16[128,512]{1,0:T(8,128)(2,1)S(1)}, bf16[128,512]{1,0:T(8,128)(2,1)S(1)}, u32[]{:S(2)}, u32[]{:S(2)}) collective-permute-start(bf16[128,512]{1,0:T(8,128)(2,1)S(1)} %get-tuple-element.19), channel_id=1, source_target_pairs={{0,16},{16,32},{32,48},{48,64},{64,80},{80,96},{96,112},{112,128},... | collective-permute-start | bytes 393224 | tf_op jit(solution)/shard_map/ppermute | solution.py:12
  26.5 13.9 %collective-permute-start.3 = (bf16[128,512]{1,0:T(8,128)(2,1)S(1)}, bf16[128,512]{1,0:T(8,128)(2,1)S(1)}, u32[]{:S(2)}, u32[]{:S(2)}) collective-permute-start(bf16[128,512]{1,0:T(8,128)(2,1)S(1)} %get-tuple-element.20), channel_id=1, source_target_pairs={{0,1},{1,2},{2,3},{3,4},{4,5},{5,6},{6,7},{7,8},{8,9},{9,10},{10,1... | collective-permute-start | bytes 393224 | tf_op jit(solution)/shard_map/ppermute | solution.py:12
  34.4 17.7 %collective-permute-start.16 = (bf16[128,512]{1,0:T(8,128)(2,1)S(1)}, bf16[128,512]{1,0:T(8,128)(2,1)S(1)}, u32[]{:S(2)}, u32[]{:S(2)}) collective-permute-start(bf16[128,512]{1,0:T(8,128)(2,1)S(1)} %get-tuple-element.33), channel_id=1, source_target_pairs={{0,16},{16,32},{32,48},{48,64},{64,80},{80,96},{96,112},{112,128},... | collective-permute-start | bytes 393224 | tf_op jit(solution)/shard_map/ppermute | solution.py:12
  38.2 14.0 %collective-permute-start.17 = (bf16[128,512]{1,0:T(8,128)(2,1)S(1)}, bf16[128,512]{1,0:T(8,128)(2,1)S(1)}, u32[]{:S(2)}, u32[]{:S(2)}) collective-permute-start(bf16[128,512]{1,0:T(8,128)(2,1)S(1)} %get-tuple-element.34), channel_id=1, source_target_pairs={{0,1},{1,2},{2,3},{3,4},{4,5},{5,6},{6,7},{7,8},{8,9},{9,10},{10,1... | collective-permute-start | bytes 393224 | tf_op jit(solution)/shard_map/ppermute | solution.py:12
  41.2 16.7 %collective-permute-start.4 = (bf16[128,512]{1,0:T(8,128)(2,1)S(1)}, bf16[128,512]{1,0:T(8,128)(2,1)S(1)}, u32[]{:S(2)}, u32[]{:S(2)}) collective-permute-start(bf16[128,512]{1,0:T(8,128)(2,1)S(1)} %get-tuple-element.17), channel_id=1, source_target_pairs={{0,16},{16,32},{32,48},{48,64},{64,80},{80,96},{96,112},{112,128},... | collective-permute-start | bytes 393224 | tf_op jit(solution)/shard_map/ppermute | solution.py:12
  44.4 13.6 %collective-permute-start.5 = (bf16[128,512]{1,0:T(8,128)(2,1)S(1)}, bf16[128,512]{1,0:T(8,128)(2,1)S(1)}, u32[]{:S(2)}, u32[]{:S(2)}) collective-permute-start(bf16[128,512]{1,0:T(8,128)(2,1)S(1)} %get-tuple-element.18), channel_id=1, source_target_pairs={{0,1},{1,2},{2,3},{3,4},{4,5},{5,6},{6,7},{7,8},{8,9},{9,10},{10,1... | collective-permute-start | bytes 393224 | tf_op jit(solution)/shard_map/ppermute | solution.py:12
  53.0 15.6 %collective-permute-start.18 = (bf16[128,512]{1,0:T(8,128)(2,1)S(1)}, bf16[128,512]{1,0:T(8,128)(2,1)S(1)}, u32[]{:S(2)}, u32[]{:S(2)}) collective-permute-start(bf16[128,512]{1,0:T(8,128)(2,1)S(1)} %get-tuple-element.31), channel_id=1, source_target_pairs={{0,16},{16,32},{32,48},{48,64},{64,80},{80,96},{96,112},{112,128},... | collective-permute-start | bytes 393224 | tf_op jit(solution)/shard_map/ppermute | solution.py:12
  55.7 12.9 %collective-permute-start.19 = (bf16[128,512]{1,0:T(8,128)(2,1)S(1)}, bf16[128,512]{1,0:T(8,128)(2,1)S(1)}, u32[]{:S(2)}, u32[]{:S(2)}) collective-permute-start(bf16[128,512]{1,0:T(8,128)(2,1)S(1)} %get-tuple-element.32), channel_id=1, source_target_pairs={{0,1},{1,2},{2,3},{3,4},{4,5},{5,6},{6,7},{7,8},{8,9},{9,10},{10,1... | collective-permute-start | bytes 393224 | tf_op jit(solution)/shard_map/ppermute | solution.py:12
  58.7 15.5 %collective-permute-start.6 = (bf16[128,512]{1,0:T(8,128)(2,1)S(1)}, bf16[128,512]{1,0:T(8,128)(2,1)S(1)}, u32[]{:S(2)}, u32[]{:S(2)}) collective-permute-start(bf16[128,512]{1,0:T(8,128)(2,1)S(1)} %get-tuple-element.15), channel_id=1, source_target_pairs={{0,16},{16,32},{32,48},{48,64},{64,80},{80,96},{96,112},{112,128},... | collective-permute-start | bytes 393224 | tf_op jit(solution)/shard_map/ppermute | solution.py:12
  61.6 12.7 %collective-permute-start.7 = (bf16[128,512]{1,0:T(8,128)(2,1)S(1)}, bf16[128,512]{1,0:T(8,128)(2,1)S(1)}, u32[]{:S(2)}, u32[]{:S(2)}) collective-permute-start(bf16[128,512]{1,0:T(8,128)(2,1)S(1)} %get-tuple-element.16), channel_id=1, source_target_pairs={{0,1},{1,2},{2,3},{3,4},{4,5},{5,6},{6,7},{7,8},{8,9},{9,10},{10,1... | collective-permute-start | bytes 393224 | tf_op jit(solution)/shard_map/ppermute | solution.py:12
  75.1 11.8 %collective-permute-start.8 = (bf16[128,512]{1,0:T(8,128)(2,1)S(1)}, bf16[128,512]{1,0:T(8,128)(2,1)S(1)}, u32[]{:S(2)}, u32[]{:S(2)}) collective-permute-start(bf16[128,512]{1,0:T(8,128)(2,1)S(1)} %get-tuple-element.13), channel_id=1, source_target_pairs={{16,0},{32,16},{48,32},{64,48},{80,64},{96,80},{112,96},{128,112},... | collective-permute-start | bytes 393224 | tf_op jit(solution)/shard_map/ppermute | solution.py:12
  77.8 12.3 %collective-permute-start.9 = (bf16[128,512]{1,0:T(8,128)(2,1)S(1)}, bf16[128,512]{1,0:T(8,128)(2,1)S(1)}, u32[]{:S(2)}, u32[]{:S(2)}) collective-permute-start(bf16[128,512]{1,0:T(8,128)(2,1)S(1)} %get-tuple-element.14), channel_id=1, source_target_pairs={{1,0},{2,1},{3,2},{4,3},{5,4},{6,5},{7,6},{8,7},{9,8},{10,9},{11,1... | collective-permute-start | bytes 393224 | tf_op jit(solution)/shard_map/ppermute | solution.py:12
  81.3 15.1 %collective-permute-start.22 = (bf16[128,512]{1,0:T(8,128)(2,1)S(1)}, bf16[128,512]{1,0:T(8,128)(2,1)S(1)}, u32[]{:S(2)}, u32[]{:S(2)}) collective-permute-start(bf16[128,512]{1,0:T(8,128)(2,1)S(1)} %get-tuple-element.27), channel_id=1, source_target_pairs={{16,0},{32,16},{48,32},{64,48},{80,64},{96,80},{112,96},{128,112},... | collective-permute-start | bytes 393224 | tf_op jit(solution)/shard_map/ppermute | solution.py:12
  84.7 12.3 %collective-permute-start.23 = (bf16[128,512]{1,0:T(8,128)(2,1)S(1)}, bf16[128,512]{1,0:T(8,128)(2,1)S(1)}, u32[]{:S(2)}, u32[]{:S(2)}) collective-permute-start(bf16[128,512]{1,0:T(8,128)(2,1)S(1)} %get-tuple-element.28), channel_id=1, source_target_pairs={{1,0},{2,1},{3,2},{4,3},{5,4},{6,5},{7,6},{8,7},{9,8},{10,9},{11,1... | collective-permute-start | bytes 393224 | tf_op jit(solution)/shard_map/ppermute | solution.py:12
  94.5 12.3 %collective-permute-start.11 = (bf16[128,512]{1,0:T(8,128)(2,1)S(1)}, bf16[128,512]{1,0:T(8,128)(2,1)S(1)}, u32[]{:S(2)}, u32[]{:S(2)}) collective-permute-start(bf16[128,512]{1,0:T(8,128)(2,1)S(1)} %get-tuple-element.12), channel_id=1, source_target_pairs={{1,0},{2,1},{3,2},{4,3},{5,4},{6,5},{7,6},{8,7},{9,8},{10,9},{11,1... | collective-permute-start | bytes 393224 | tf_op jit(solution)/shard_map/ppermute | solution.py:12
  97.8 14.1 %collective-permute-start.24 = (bf16[128,512]{1,0:T(8,128)(2,1)S(1)}, bf16[128,512]{1,0:T(8,128)(2,1)S(1)}, u32[]{:S(2)}, u32[]{:S(2)}) collective-permute-start(bf16[128,512]{1,0:T(8,128)(2,1)S(1)} %get-tuple-element.25), channel_id=1, source_target_pairs={{16,0},{32,16},{48,32},{64,48},{80,64},{96,80},{112,96},{128,112},... | collective-permute-start | bytes 393224 | tf_op jit(solution)/shard_map/ppermute | solution.py:12
  100.0 12.3 %collective-permute-start.25 = (bf16[128,512]{1,0:T(8,128)(2,1)S(1)}, bf16[128,512]{1,0:T(8,128)(2,1)S(1)}, u32[]{:S(2)}, u32[]{:S(2)}) collective-permute-start(bf16[128,512]{1,0:T(8,128)(2,1)S(1)} %get-tuple-element.26), channel_id=1, source_target_pairs={{1,0},{2,1},{3,2},{4,3},{5,4},{6,5},{7,6},{8,7},{9,8},{10,9},{11,1... | collective-permute-start | bytes 393224 | tf_op jit(solution)/shard_map/ppermute | solution.py:12
  107.6 12.1 %collective-permute-start.12 = (bf16[128,512]{1,0:T(8,128)(2,1)S(1)}, bf16[128,512]{1,0:T(8,128)(2,1)S(1)}, u32[]{:S(2)}, u32[]{:S(2)}) collective-permute-start(bf16[128,512]{1,0:T(8,128)(2,1)S(1)} %get-tuple-element.9), channel_id=1, source_target_pairs={{16,0},{32,16},{48,32},{64,48},{80,64},{96,80},{112,96},{128,112},... | collective-permute-start | bytes 393224 | tf_op jit(solution)/shard_map/ppermute | solution.py:12
  109.8 12.4 %collective-permute-start.13 = (bf16[128,512]{1,0:T(8,128)(2,1)S(1)}, bf16[128,512]{1,0:T(8,128)(2,1)S(1)}, u32[]{:S(2)}, u32[]{:S(2)}) collective-permute-start(bf16[128,512]{1,0:T(8,128)(2,1)S(1)} %get-tuple-element.10), channel_id=1, source_target_pairs={{1,0},{2,1},{3,2},{4,3},{5,4},{6,5},{7,6},{8,7},{9,8},{10,9},{11,1... | collective-permute-start | bytes 393224 | tf_op jit(solution)/shard_map/ppermute | solution.py:12
  117.7 12.3 %collective-permute-start.27 = (bf16[128,512]{1,0:T(8,128)(2,1)S(1)}, bf16[128,512]{1,0:T(8,128)(2,1)S(1)}, u32[]{:S(2)}, u32[]{:S(2)}) collective-permute-start(bf16[128,512]{1,0:T(8,128)(2,1)S(1)} %get-tuple-element.24), channel_id=1, source_target_pairs={{1,0},{2,1},{3,2},{4,3},{5,4},{6,5},{7,6},{8,7},{9,8},{10,9},{11,1... | collective-permute-start | bytes 393224 | tf_op jit(solution)/shard_map/ppermute | solution.py:12
  (7 other events, 78.6 us)
where the time goes:
time: 134 us; the launch traced here: 133 us
  starting transfers between devices  94 us (70%)
  waiting for transfers between devices  19.5 us (15%)
  matrix products  17 us (13%)
  local copies, waits for them, and re-layouts  2.24 us (2%)
    ppermute x28, starting transfers between devices, from_behind(): return lax.ppermute(array, axis, pairs)  94 us
    ppermute x28, waiting for transfers between devices, from_behind(): return lax.ppermute(array, axis, pairs)  19.5 us
    dot_general x15, matrix products, project(): jnp.dot(state, weights[:, low:low + width], preferred_element_type=jnp.fl...  17 us
  transfers between devices with their start and end apart: 28, of which 6 were waited for; matrix products, arithmetic and copies ran while one was open for 8% of the time, Pallas kernels for 0%

commit v1 on v0

v1 whole, which is shorter than its diff:
```python
import jax
import jax.numpy as jnp
from jax import lax
from jax.sharding import PartitionSpec as P


F32, BF16 = jnp.float32, jnp.bfloat16
TICKS, TURN = 8, 4


def hop(array, axis, by, parity):
    nx, ny = lax.axis_size("gx"), lax.axis_size("gy")
    pairs = []
    for i in range(nx):
        for j in range(ny):
            a, b = (i + by, j) if axis == "gx" else (i, j + by)
            if (i + j) % 2 == parity and 0 <= a < nx and 0 <= b < ny:
                pairs.append((i * ny + j, a * ny + b))
    return lax.ppermute(array, ("gx", "gy"), pairs)


def dot(a, b):
    return jnp.dot(a, b, preferred_element_type=F32)


def cat(x, y):
    return jnp.concatenate([x, y], axis=1)


def on_device(maps, sources, traces):
    w = maps[0, 0]
    src = sources[0, 0]
    state = traces[0, 0]
    h = w.shape[0] // 2
    f = h // 2
    en = state[:, h:]
    got = [None, None]

    def send(tick, chain, value):
        o = value.astype(BF16)
        by = 1 if tick < TURN else -1
        parity = (tick + chain) % 2
        x = hop(o[:, :f], "gx", by, parity)
        y = hop(o[:, f:], "gy", by, parity)
        got[chain] = cat(x, y)

    def product(chain, block, constant):
        return dot(got[chain], block) + constant

    down, up = w[:h, h:], w[h:, :h]
    first = dot(state, w[:, h:]) + src[:, h:]
    c_en = dot(en, w[h:, h:]) + src[:, h:]
    q = dot(en, up)
    for tick in range(TURN):
        for chain in range(2):
            send(tick, chain, first if tick == 0 else product(chain, down, c_en))
    one, ws = got[0], got[0] + got[1]
    send(TURN, 0, dot(one, w[:h, :h]) + (src[:, :h] + q))
    c_ws = dot(ws, w[:h, :h]) + src[:, :h]
    send(TURN, 1, c_ws + q)
    c_out = cat(c_ws, dot(ws, down) + src[:, h:])
    for tick in range(TURN + 1, TICKS - 1):
        for chain in range(2):
            send(tick, chain, product(chain, up, c_ws))
    result = (dot(got[0] + got[1], w[h:]) + c_out).astype(BF16)
    return result[None, None]


def solution(mesh):
    spec = P("gx", "gy", None, None)
    return jax.shard_map(on_device, mesh=mesh, in_specs=(spec, spec, spec), out_specs=spec, check_vma=False)
```

time: 134 us -> 132 us (0.985)
  the two profiles are of different devices: /device:TPU:61 before, /device:TPU:57 now
where the time goes in v1:
time: 132 us; the launch traced here: 131 us
  starting transfers between devices  62.8 us (48%)
  waiting for transfers between devices  48.1 us (36%)
  matrix products  18.8 us (14%)
    ppermute x28, starting transfers between devices, hop(): return lax.ppermute(array, ('gx', 'gy'), pairs)  62.8 us
    ppermute x28, waiting for transfers between devices, hop(): return lax.ppermute(array, ('gx', 'gy'), pairs)  48.1 us
    dot_general x17, matrix products, dot(): return jnp.dot(a, b, preferred_element_type=F32)  18.8 us
  transfers between devices with their start and end apart: 28, of which 9 were waited for; matrix products, arithmetic and copies ran while one was open for 9% of the time, Pallas kernels for 0%

profile of v1, /device:TPU:57, one launch (start us, length us, event | category | flops | bytes accessed | tf_op | source)
XLA Modules:
  0.0 130.9 jit_solution(1029743012966004796)
XLA Ops:
  0.0 4.2 %fusion.32 = bf16[256,1024]{1,0:T(8,128)(2,1)S(1)} fusion(bf16[2048,2048]{1,0:T(8,128)(2,1)} %bitcast.17, f32[256,2048]{1,0:T(8,128)} %bitcast.33, bf16[1,1,256,2048]{3,2,1,0:T(8,128)(2,1)} %param.5), kind=kOutput, calls=%fused_computation.29 | convolution fusion | flops 1074266112 | bytes 6815744 | tf_op jit(solution)/shard_map/dot_general | solution.py:23
  4.3 3.3 %collective-permute-start.10 = (bf16[256,512]{1,0:T(8,128)(2,1)S(1)}, bf16[256,512]{1,0:T(8,128)(2,1)S(1)}, u32[]{:S(2)}, u32[]{:S(2)}) collective-permute-start(bf16[256,512]{1,0:T(8,128)(2,1)S(1)} %get-tuple-element.29), channel_id=1, source_target_pairs={{1,17},{3,19},{5,21},{7,23},{9,25},{11,27},{13,29},{15,31},{16,32}... | collective-permute-start | bytes 786440 | tf_op jit(solution)/shard_map/ppermute | solution.py:19
  8.8 10.5 %collective-permute-start.11 = (bf16[256,512]{1,0:T(8,128)(2,1)S(1)}, bf16[256,512]{1,0:T(8,128)(2,1)S(1)}, u32[]{:S(2)}, u32[]{:S(2)}) collective-permute-start(bf16[256,512]{1,0:T(8,128)(2,1)S(1)} %get-tuple-element.30), channel_id=1, source_target_pairs={{1,2},{3,4},{5,6},{7,8},{9,10},{11,12},{13,14},{16,17},{18,19},{20... | collective-permute-start | bytes 786440 | tf_op jit(solution)/shard_map/ppermute | solution.py:19
  20.7 1.9 %fusion.26 = f32[256,1024]{1,0:T(8,128)S(1)} fusion(bf16[2048,2048]{1,0:T(8,128)(2,1)S(1)} %bitcast.18, f32[256,2048]{1,0:T(8,128)} %bitcast.34, bf16[256,2048]{1,0:T(8,128)(2,1)S(1)} %bitcast.38), kind=kOutput, calls=%fused_computation.16 | convolution fusion | flops 537133056 | bytes 4718592 | tf_op jit(solution)/shard_map/dot_general | solution.py:23
  22.7 2.8 %collective-permute-done.11 = bf16[256,512]{1,0:T(8,128)(2,1)S(1)} collective-permute-done((bf16[256,512]{1,0:T(8,128)(2,1)S(1)}, bf16[256,512]{1,0:T(8,128)(2,1)S(1)}, u32[]{:S(2)}, u32[]{:S(2)}) %collective-permute-start.11) | collective-permute-done | bytes 262176 | tf_op jit(solution)/shard_map/ppermute | solution.py:19
  29.7 2.9 %collective-permute-start.2 = (bf16[256,512]{1,0:T(8,128)(2,1)S(1)}, bf16[256,512]{1,0:T(8,128)(2,1)S(1)}, u32[]{:S(2)}, u32[]{:S(2)}) collective-permute-start(bf16[256,512]{1,0:T(8,128)(2,1)S(1)} %get-tuple-element.27), channel_id=1, source_target_pairs={{1,17},{3,19},{5,21},{7,23},{9,25},{11,27},{13,29},{15,31},{16,32}... | collective-permute-start | bytes 786440 | tf_op jit(solution)/shard_map/ppermute | solution.py:19
  32.6 8.9 %collective-permute-start.3 = (bf16[256,512]{1,0:T(8,128)(2,1)S(1)}, bf16[256,512]{1,0:T(8,128)(2,1)S(1)}, u32[]{:S(2)}, u32[]{:S(2)}) collective-permute-start(bf16[256,512]{1,0:T(8,128)(2,1)S(1)} %get-tuple-element.28), channel_id=1, source_target_pairs={{1,2},{3,4},{5,6},{7,8},{9,10},{11,12},{13,14},{16,17},{18,19},{20... | collective-permute-start | bytes 786440 | tf_op jit(solution)/shard_map/ppermute | solution.py:19
  42.3 1.3 collective-permute-start.14
  43.6 1.3 collective-permute-start.15
  44.9 3.6 %collective-permute-done.3 = bf16[256,512]{1,0:T(8,128)(2,1)S(1)} collective-permute-done((bf16[256,512]{1,0:T(8,128)(2,1)S(1)}, bf16[256,512]{1,0:T(8,128)(2,1)S(1)}, u32[]{:S(2)}, u32[]{:S(2)}) %collective-permute-start.3) | collective-permute-done | bytes 262176 | tf_op jit(solution)/shard_map/ppermute | solution.py:19
  55.4 3.2 %collective-permute-done.4 = bf16[256,512]{1,0:T(8,128)(2,1)S(1)} collective-permute-done((bf16[256,512]{1,0:T(8,128)(2,1)S(1)}, bf16[256,512]{1,0:T(8,128)(2,1)S(1)}, u32[]{:S(2)}, u32[]{:S(2)}) %collective-permute-start.4) | collective-permute-done | bytes 262176 | tf_op jit(solution)/shard_map/ppermute | solution.py:19
  59.4 7.3 %collective-permute-start.7 = (bf16[256,512]{1,0:T(8,128)(2,1)S(1)}, bf16[256,512]{1,0:T(8,128)(2,1)S(1)}, u32[]{:S(2)}, u32[]{:S(2)}) collective-permute-start(bf16[256,512]{1,0:T(8,128)(2,1)S(1)} %get-tuple-element.23), channel_id=1, source_target_pairs={{1,2},{3,4},{5,6},{7,8},{9,10},{11,12},{13,14},{16,17},{18,19},{20... | collective-permute-start | bytes 786440 | tf_op jit(solution)/shard_map/ppermute | solution.py:19
  66.7 1.4 %collective-permute-start.6 = (bf16[256,512]{1,0:T(8,128)(2,1)S(1)}, bf16[256,512]{1,0:T(8,128)(2,1)S(1)}, u32[]{:S(2)}, u32[]{:S(2)}) collective-permute-start(bf16[256,512]{1,0:T(8,128)(2,1)S(1)} %get-tuple-element.24), channel_id=1, source_target_pairs={{1,17},{3,19},{5,21},{7,23},{9,25},{11,27},{13,29},{15,31},{16,32}... | collective-permute-start | bytes 786440 | tf_op jit(solution)/shard_map/ppermute | solution.py:19
  68.9 2.6 %collective-permute-done.6 = bf16[256,512]{1,0:T(8,128)(2,1)S(1)} collective-permute-done((bf16[256,512]{1,0:T(8,128)(2,1)S(1)}, bf16[256,512]{1,0:T(8,128)(2,1)S(1)}, u32[]{:S(2)}, u32[]{:S(2)}) %collective-permute-start.6) | collective-permute-done | bytes 262176 | tf_op jit(solution)/shard_map/ppermute | solution.py:19
  72.4 1.3 collective-permute-start.22
  73.7 1.3 collective-permute-start.23
  82.9 9.2 %collective-permute-done.9 = bf16[256,512]{1,0:T(8,128)(2,1)S(1)} collective-permute-done((bf16[256,512]{1,0:T(8,128)(2,1)S(1)}, bf16[256,512]{1,0:T(8,128)(2,1)S(1)}, u32[]{:S(2)}, u32[]{:S(2)}) %collective-permute-start.9) | collective-permute-done | bytes 262176 | tf_op jit(solution)/shard_map/ppermute | solution.py:19
  92.9 1.3 collective-permute-start.18
  94.2 1.3 collective-permute-start.19
  95.5 11.1 %collective-permute-done.25 = bf16[256,512]{1,0:T(8,128)(2,1)S(1)} collective-permute-done((bf16[256,512]{1,0:T(8,128)(2,1)S(1)}, bf16[256,512]{1,0:T(8,128)(2,1)S(1)}, u32[]{:S(2)}, u32[]{:S(2)}) %collective-permute-start.25) | collective-permute-done | bytes 262176 | tf_op jit(solution)/shard_map/ppermute | solution.py:19
  107.4 1.3 collective-permute-start.26
  114.2 3.7 %collective-permute-done.20 = bf16[256,512]{1,0:T(8,128)(2,1)S(1)} collective-permute-done((bf16[256,512]{1,0:T(8,128)(2,1)S(1)}, bf16[256,512]{1,0:T(8,128)(2,1)S(1)}, u32[]{:S(2)}, u32[]{:S(2)}) %collective-permute-start.20) | collective-permute-done | bytes 262176 | tf_op jit(solution)/shard_map/ppermute | solution.py:19
  118.0 10.7 %collective-permute-done.21 = bf16[256,512]{1,0:T(8,128)(2,1)S(1)} collective-permute-done((bf16[256,512]{1,0:T(8,128)(2,1)S(1)}, bf16[256,512]{1,0:T(8,128)(2,1)S(1)}, u32[]{:S(2)}, u32[]{:S(2)}) %collective-permute-start.21) | collective-permute-done | bytes 262176 | tf_op jit(solution)/shard_map/ppermute | solution.py:19
  128.7 2.2 %fusion.11 = bf16[1,1,256,2048]{3,2,1,0:T(8,128)(2,1)} fusion(bf16[1,1,2048,2048]{3,2,1,0:T(8,128)(2,1)S(1)} %copy-done, f32[256,1024]{1,0:T(8,128)S(1)} %convolution_add_fusion, f32[256,1024]{1,0:T(8,128)S(1)} %get-tuple-element.32, bf16[256,512]{1,0:T(8,128)(2,1)S(1)} %collective-permute-done.21, bf16[256,512]{1,0:T(8,128)(2,1)S(1)} %collective-permute-done.20, ...), kind=kOutput, calls=%fused_computation.7 | convolution fusion | flops 1077411840 | bytes 8388608 | tf_op jit(solution)/shard_map/dot_general | solution.py:23
  (70 shorter events, 31.5 us)
Async XLA Ops:
  4.3 18.4 %collective-permute-start.10 = (bf16[256,512]{1,0:T(8,128)(2,1)S(1)}, bf16[256,512]{1,0:T(8,128)(2,1)S(1)}, u32[]{:S(2)}, u32[]{:S(2)}) collective-permute-start(bf16[256,512]{1,0:T(8,128)(2,1)S(1)} %get-tuple-element.29), channel_id=1, source_target_pairs={{1,17},{3,19},{5,21},{7,23},{9,25},{11,27},{13,29},{15,31},{16,32}... | collective-permute-start | bytes 786440 | tf_op jit(solution)/shard_map/ppermute | solution.py:19
  7.5 21.4 %collective-permute-start = (bf16[256,512]{1,0:T(8,128)(2,1)S(1)}, bf16[256,512]{1,0:T(8,128)(2,1)S(1)}, u32[]{:S(2)}, u32[]{:S(2)}) collective-permute-start(bf16[256,512]{1,0:T(8,128)(2,1)S(1)} %get-tuple-element.29), channel_id=1, source_target_pairs={{0,16},{2,18},{4,20},{6,22},{8,24},{10,26},{12,28},{14,30},{17,33}... | collective-permute-start | bytes 786440 | tf_op jit(solution)/shard_map/ppermute | solution.py:19
  8.8 16.6 %collective-permute-start.11 = (bf16[256,512]{1,0:T(8,128)(2,1)S(1)}, bf16[256,512]{1,0:T(8,128)(2,1)S(1)}, u32[]{:S(2)}, u32[]{:S(2)}) collective-permute-start(bf16[256,512]{1,0:T(8,128)(2,1)S(1)} %get-tuple-element.30), channel_id=1, source_target_pairs={{1,2},{3,4},{5,6},{7,8},{9,10},{11,12},{13,14},{16,17},{18,19},{20... | collective-permute-start | bytes 786440 | tf_op jit(solution)/shard_map/ppermute | solution.py:19
  19.4 9.5 %collective-permute-start.1 = (bf16[256,512]{1,0:T(8,128)(2,1)S(1)}, bf16[256,512]{1,0:T(8,128)(2,1)S(1)}, u32[]{:S(2)}, u32[]{:S(2)}) collective-permute-start(bf16[256,512]{1,0:T(8,128)(2,1)S(1)} %get-tuple-element.30), channel_id=1, source_target_pairs={{0,1},{2,3},{4,5},{6,7},{8,9},{10,11},{12,13},{14,15},{17,18},{19,... | collective-permute-start | bytes 786440 | tf_op jit(solution)/shard_map/ppermute | solution.py:19
  26.3 15.2 %collective-permute-start.12 = (bf16[256,512]{1,0:T(8,128)(2,1)S(1)}, bf16[256,512]{1,0:T(8,128)(2,1)S(1)}, u32[]{:S(2)}, u32[]{:S(2)}) collective-permute-start(bf16[256,512]{1,0:T(8,128)(2,1)S(1)} %get-tuple-element.21), channel_id=1, source_target_pairs={{0,16},{2,18},{4,20},{6,22},{8,24},{10,26},{12,28},{14,30},{17,33}... | collective-permute-start | bytes 786440 | tf_op jit(solution)/shard_map/ppermute | solution.py:19
  27.6 13.9 %collective-permute-start.13 = (bf16[256,512]{1,0:T(8,128)(2,1)S(1)}, bf16[256,512]{1,0:T(8,128)(2,1)S(1)}, u32[]{:S(2)}, u32[]{:S(2)}) collective-permute-start(bf16[256,512]{1,0:T(8,128)(2,1)S(1)} %get-tuple-element.22), channel_id=1, source_target_pairs={{0,1},{2,3},{4,5},{6,7},{8,9},{10,11},{12,13},{14,15},{17,18},{19,... | collective-permute-start | bytes 786440 | tf_op jit(solution)/shard_map/ppermute | solution.py:19
  29.7 15.2 %collective-permute-start.2 = (bf16[256,512]{1,0:T(8,128)(2,1)S(1)}, bf16[256,512]{1,0:T(8,128)(2,1)S(1)}, u32[]{:S(2)}, u32[]{:S(2)}) collective-permute-start(bf16[256,512]{1,0:T(8,128)(2,1)S(1)} %get-tuple-element.27), channel_id=1, source_target_pairs={{1,17},{3,19},{5,21},{7,23},{9,25},{11,27},{13,29},{15,31},{16,32}... | collective-permute-start | bytes 786440 | tf_op jit(solution)/shard_map/ppermute | solution.py:19
  32.6 16.0 %collective-permute-start.3 = (bf16[256,512]{1,0:T(8,128)(2,1)S(1)}, bf16[256,512]{1,0:T(8,128)(2,1)S(1)}, u32[]{:S(2)}, u32[]{:S(2)}) collective-permute-start(bf16[256,512]{1,0:T(8,128)(2,1)S(1)} %get-tuple-element.28), channel_id=1, source_target_pairs={{1,2},{3,4},{5,6},{7,8},{9,10},{11,12},{13,14},{16,17},{18,19},{20... | collective-permute-start | bytes 786440 | tf_op jit(solution)/shard_map/ppermute | solution.py:19
  42.3 9.7 %collective-permute-start.14 = (bf16[256,512]{1,0:T(8,128)(2,1)S(1)}, bf16[256,512]{1,0:T(8,128)(2,1)S(1)}, u32[]{:S(2)}, u32[]{:S(2)}) collective-permute-start(bf16[256,512]{1,0:T(8,128)(2,1)S(1)} %get-tuple-element.19), channel_id=1, source_target_pairs={{1,17},{3,19},{5,21},{7,23},{9,25},{11,27},{13,29},{15,31},{16,32}... | collective-permute-start | bytes 786440 | tf_op jit(solution)/shard_map/ppermute | solution.py:19
  43.6 8.4 %collective-permute-start.15 = (bf16[256,512]{1,0:T(8,128)(2,1)S(1)}, bf16[256,512]{1,0:T(8,128)(2,1)S(1)}, u32[]{:S(2)}, u32[]{:S(2)}) collective-permute-start(bf16[256,512]{1,0:T(8,128)(2,1)S(1)} %get-tuple-element.20), channel_id=1, source_target_pairs={{1,2},{3,4},{5,6},{7,8},{9,10},{11,12},{13,14},{16,17},{18,19},{20... | collective-permute-start | bytes 786440 | tf_op jit(solution)/shard_map/ppermute | solution.py:19
  49.4 9.2 %collective-permute-start.4 = (bf16[256,512]{1,0:T(8,128)(2,1)S(1)}, bf16[256,512]{1,0:T(8,128)(2,1)S(1)}, u32[]{:S(2)}, u32[]{:S(2)}) collective-permute-start(bf16[256,512]{1,0:T(8,128)(2,1)S(1)} %get-tuple-element.25), channel_id=1, source_target_pairs={{0,16},{2,18},{4,20},{6,22},{8,24},{10,26},{12,28},{14,30},{17,33}... | collective-permute-start | bytes 786440 | tf_op jit(solution)/shard_map/ppermute | solution.py:19
  50.7 7.9 %collective-permute-start.5 = (bf16[256,512]{1,0:T(8,128)(2,1)S(1)}, bf16[256,512]{1,0:T(8,128)(2,1)S(1)}, u32[]{:S(2)}, u32[]{:S(2)}) collective-permute-start(bf16[256,512]{1,0:T(8,128)(2,1)S(1)} %get-tuple-element.26), channel_id=1, source_target_pairs={{0,1},{2,3},{4,5},{6,7},{8,9},{10,11},{12,13},{14,15},{17,18},{19,... | collective-permute-start | bytes 786440 | tf_op jit(solution)/shard_map/ppermute | solution.py:19
  52.8 18.7 %collective-permute-start.16 = (bf16[256,512]{1,0:T(8,128)(2,1)S(1)}, bf16[256,512]{1,0:T(8,128)(2,1)S(1)}, u32[]{:S(2)}, u32[]{:S(2)}) collective-permute-start(bf16[256,512]{1,0:T(8,128)(2,1)S(1)} %get-tuple-element.17), channel_id=1, source_target_pairs={{0,16},{2,18},{4,20},{6,22},{8,24},{10,26},{12,28},{14,30},{17,33}... | collective-permute-start | bytes 786440 | tf_op jit(solution)/shard_map/ppermute | solution.py:19
  54.1 17.4 %collective-permute-start.17 = (bf16[256,512]{1,0:T(8,128)(2,1)S(1)}, bf16[256,512]{1,0:T(8,128)(2,1)S(1)}, u32[]{:S(2)}, u32[]{:S(2)}) collective-permute-start(bf16[256,512]{1,0:T(8,128)(2,1)S(1)} %get-tuple-element.18), channel_id=1, source_target_pairs={{0,1},{2,3},{4,5},{6,7},{8,9},{10,11},{12,13},{14,15},{17,18},{19,... | collective-permute-start | bytes 786440 | tf_op jit(solution)/shard_map/ppermute | solution.py:19
  59.4 12.1 %collective-permute-start.7 = (bf16[256,512]{1,0:T(8,128)(2,1)S(1)}, bf16[256,512]{1,0:T(8,128)(2,1)S(1)}, u32[]{:S(2)}, u32[]{:S(2)}) collective-permute-start(bf16[256,512]{1,0:T(8,128)(2,1)S(1)} %get-tuple-element.23), channel_id=1, source_target_pairs={{1,2},{3,4},{5,6},{7,8},{9,10},{11,12},{13,14},{16,17},{18,19},{20... | collective-permute-start | bytes 786440 | tf_op jit(solution)/shard_map/ppermute | solution.py:19
  75.8 7.1 %collective-permute-start.8 = (bf16[256,512]{1,0:T(8,128)(2,1)S(1)}, bf16[256,512]{1,0:T(8,128)(2,1)S(1)}, u32[]{:S(2)}, u32[]{:S(2)}) collective-permute-start(bf16[256,512]{1,0:T(8,128)(2,1)S(1)} %get-tuple-element.15), channel_id=1, source_target_pairs={{17,1},{19,3},{21,5},{23,7},{25,9},{27,11},{29,13},{31,15},{32,16}... | collective-permute-start | bytes 786440 | tf_op jit(solution)/shard_map/ppermute | solution.py:19
  77.1 15.0 %collective-permute-start.9 = (bf16[256,512]{1,0:T(8,128)(2,1)S(1)}, bf16[256,512]{1,0:T(8,128)(2,1)S(1)}, u32[]{:S(2)}, u32[]{:S(2)}) collective-permute-start(bf16[256,512]{1,0:T(8,128)(2,1)S(1)} %get-tuple-element.16), channel_id=1, source_target_pairs={{2,1},{4,3},{6,5},{8,7},{10,9},{12,11},{14,13},{17,16},{19,18},{21... | collective-permute-start | bytes 786440 | tf_op jit(solution)/shard_map/ppermute | solution.py:19
  79.2 16.4 %collective-permute-start.24 = (bf16[256,512]{1,0:T(8,128)(2,1)S(1)}, bf16[256,512]{1,0:T(8,128)(2,1)S(1)}, u32[]{:S(2)}, u32[]{:S(2)}) collective-permute-start(bf16[256,512]{1,0:T(8,128)(2,1)S(1)} %get-tuple-element.7), channel_id=1, source_target_pairs={{17,1},{19,3},{21,5},{23,7},{25,9},{27,11},{29,13},{31,15},{32,16}... | collective-permute-start | bytes 786440 | tf_op jit(solution)/shard_map/ppermute | solution.py:19
  80.5 26.1 %collective-permute-start.25 = (bf16[256,512]{1,0:T(8,128)(2,1)S(1)}, bf16[256,512]{1,0:T(8,128)(2,1)S(1)}, u32[]{:S(2)}, u32[]{:S(2)}) collective-permute-start(bf16[256,512]{1,0:T(8,128)(2,1)S(1)} %get-tuple-element.8), channel_id=1, source_target_pairs={{2,1},{4,3},{6,5},{8,7},{10,9},{12,11},{14,13},{17,16},{19,18},{21... | collective-permute-start | bytes 786440 | tf_op jit(solution)/shard_map/ppermute | solution.py:19
  92.9 17.1 %collective-permute-start.18 = (bf16[256,512]{1,0:T(8,128)(2,1)S(1)}, bf16[256,512]{1,0:T(8,128)(2,1)S(1)}, u32[]{:S(2)}, u32[]{:S(2)}) collective-permute-start(bf16[256,512]{1,0:T(8,128)(2,1)S(1)} %get-tuple-element.13), channel_id=1, source_target_pairs={{16,0},{18,2},{20,4},{22,6},{24,8},{26,10},{28,12},{30,14},{33,17}... | collective-permute-start | bytes 786440 | tf_op jit(solution)/shard_map/ppermute | solution.py:19
  94.2 15.8 %collective-permute-start.19 = (bf16[256,512]{1,0:T(8,128)(2,1)S(1)}, bf16[256,512]{1,0:T(8,128)(2,1)S(1)}, u32[]{:S(2)}, u32[]{:S(2)}) collective-permute-start(bf16[256,512]{1,0:T(8,128)(2,1)S(1)} %get-tuple-element.14), channel_id=1, source_target_pairs={{1,0},{3,2},{5,4},{7,6},{9,8},{11,10},{13,12},{15,14},{18,17},{20,... | collective-permute-start | bytes 786440 | tf_op jit(solution)/shard_map/ppermute | solution.py:19
  107.4 6.8 %collective-permute-start.26 = (bf16[256,512]{1,0:T(8,128)(2,1)S(1)}, bf16[256,512]{1,0:T(8,128)(2,1)S(1)}, u32[]{:S(2)}, u32[]{:S(2)}) collective-permute-start(bf16[256,512]{1,0:T(8,128)(2,1)S(1)} %get-tuple-element.5), channel_id=1, source_target_pairs={{16,0},{18,2},{20,4},{22,6},{24,8},{26,10},{28,12},{30,14},{33,17}... | collective-permute-start | bytes 786440 | tf_op jit(solution)/shard_map/ppermute | solution.py:19
  110.8 7.1 %collective-permute-start.20 = (bf16[256,512]{1,0:T(8,128)(2,1)S(1)}, bf16[256,512]{1,0:T(8,128)(2,1)S(1)}, u32[]{:S(2)}, u32[]{:S(2)}) collective-permute-start(bf16[256,512]{1,0:T(8,128)(2,1)S(1)} %get-tuple-element.11), channel_id=1, source_target_pairs={{17,1},{19,3},{21,5},{23,7},{25,9},{27,11},{29,13},{31,15},{32,16}... | collective-permute-start | bytes 786440 | tf_op jit(solution)/shard_map/ppermute | solution.py:19
  112.1 16.5 %collective-permute-start.21 = (bf16[256,512]{1,0:T(8,128)(2,1)S(1)}, bf16[256,512]{1,0:T(8,128)(2,1)S(1)}, u32[]{:S(2)}, u32[]{:S(2)}) collective-permute-start(bf16[256,512]{1,0:T(8,128)(2,1)S(1)} %get-tuple-element.12), channel_id=1, source_target_pairs={{2,1},{4,3},{6,5},{8,7},{10,9},{12,11},{14,13},{17,16},{19,18},{21... | collective-permute-start | bytes 786440 | tf_op jit(solution)/shard_map/ppermute | solution.py:19
  (7 other events, 67.2 us)

commit v2 on v1

--- a/solution.py
+++ b/solution.py
@@ -36,33 +36,42 @@
     en = state[:, h:]
     got = [None, None]
 
-    def send(tick, chain, value):
-        o = value.astype(BF16)
+    def send(tick, chain, x, y):
         by = 1 if tick < TURN else -1
         parity = (tick + chain) % 2
-        x = hop(o[:, :f], "gx", by, parity)
-        y = hop(o[:, f:], "gy", by, parity)
-        got[chain] = cat(x, y)
+        y = hop(y, "gy", by, parity)
+        x = hop(x, "gx", by, parity)
+        got[chain] = (x, y)
+
+    def send_both(tick, chain, value):
+        o = value.astype(BF16)
+        send(tick, chain, o[:, :f], o[:, f:])
 
     def product(chain, block, constant):
-        return dot(got[chain], block) + constant
+        return dot(cat(*got[chain]), block) + constant
 
     down, up = w[:h, h:], w[h:, :h]
-    first = dot(state, w[:, h:]) + src[:, h:]
+    north = (dot(state, w[:, h + f :]) + src[:, h + f :]).astype(BF16)
+    east = (dot(state, w[:, h : h + f]) + src[:, h : h + f]).astype(BF16)
     c_en = dot(en, w[h:, h:]) + src[:, h:]
     q = dot(en, up)
-    for tick in range(TURN):
+    for chain in range(2):
+        send(0, chain, east, north)
+    for tick in range(1, TURN):
         for chain in range(2):
-            send(tick, chain, first if tick == 0 else product(chain, down, c_en))
-    one, ws = got[0], got[0] + got[1]
-    send(TURN, 0, dot(one, w[:h, :h]) + (src[:, :h] + q))
+            send_both(tick, chain, product(chain, down, c_en))
+    one, two = cat(*got[0]), cat(*got[1])
+    ws = one + two
+    send_both(TURN, 0, dot(one, w[:h, :h]) + (src[:, :h] + q))
     c_ws = dot(ws, w[:h, :h]) + src[:, :h]
-    send(TURN, 1, c_ws + q)
+    send_both(TURN, 1, c_ws + q)
     c_out = cat(c_ws, dot(ws, down) + src[:, h:])
     for tick in range(TURN + 1, TICKS - 1):
         for chain in range(2):
-            send(tick, chain, product(chain, up, c_ws))
-    result = (dot(got[0] + got[1], w[h:]) + c_out).astype(BF16)
+            send_both(tick, chain, product(chain, up, c_ws))
+    c_out = dot(got[0][0] + got[1][0], w[h : h + f]) + c_out
+    result = dot(got[0][1] + got[1][1], w[h + f :]) + c_out
+    result = result.astype(BF16)
     return result[None, None]
 
 

time: 132 us -> 133 us (level)
  matrix products: 18.8 us -> 20.2 us
    dot_general x17 -> x19, matrix products: 18.8 us -> 20.2 us  [dot(): return jnp.dot(a, b, preferred_element_type=F32)]
  transfers between devices with their start and end apart: 28 -> 28, of which waited for: 9 -> 9; matrix products, arithmetic and copies ran while one was open for 9% -> 12% of each run, Pallas kernels for 0% -> 0%
where the time goes in v2:
time: 133 us; the launch traced here: 132 us
  starting transfers between devices  62.9 us (47%)
  waiting for transfers between devices  48.1 us (36%)
  matrix products  20.2 us (15%)
    ppermute x28, starting transfers between devices, hop(): return lax.ppermute(array, ('gx', 'gy'), pairs)  62.9 us
    ppermute x28, waiting for transfers between devices, hop(): return lax.ppermute(array, ('gx', 'gy'), pairs)  48.1 us
    dot_general x19, matrix products, dot(): return jnp.dot(a, b, preferred_element_type=F32)  20.2 us
  transfers between devices with their start and end apart: 28, of which 9 were waited for; matrix products, arithmetic and copies ran while one was open for 12% of the time, Pallas kernels for 0%

profile of v2, /device:TPU:57, one launch (start us, length us, event | category | flops | bytes accessed | tf_op | source)
XLA Modules:
  0.0 132.3 jit_solution(14298487064171585750)
XLA Ops:
  0.0 2.9 %fusion.47 = bf16[256,512]{1,0:T(8,128)(2,1)S(1)} fusion(bf16[2048,2048]{1,0:T(8,128)(2,1)} %bitcast.16, f32[256,2048]{1,0:T(8,128)} %bitcast.33, bf16[1,1,256,2048]{3,2,1,0:T(8,128)(2,1)} %param.5), kind=kOutput, calls=%fused_computation.46 | convolution fusion | flops 537133056 | bytes 3932160 | tf_op jit(solution)/shard_map/dot_general | solution.py:23
  2.9 3.4 %collective-permute-start.10 = (bf16[256,512]{1,0:T(8,128)(2,1)S(1)}, bf16[256,512]{1,0:T(8,128)(2,1)S(1)}, u32[]{:S(2)}, u32[]{:S(2)}) collective-permute-start(bf16[256,512]{1,0:T(8,128)(2,1)S(1)} %fusion.47), channel_id=1, source_target_pairs={{1,17},{3,19},{5,21},{7,23},{9,25},{11,27},{13,29},{15,31},{16,32}... | collective-permute-start | bytes 786440 | tf_op jit(solution)/shard_map/ppermute | solution.py:19
  7.6 2.7 %fusion.44 = bf16[256,512]{1,0:T(8,128)(2,1)S(1)} fusion(bf16[2048,2048]{1,0:T(8,128)(2,1)} %bitcast.17, f32[256,2048]{1,0:T(8,128)} %bitcast.34, bf16[1,1,256,2048]{3,2,1,0:T(8,128)(2,1)} %param.5), kind=kOutput, calls=%fused_computation.45 | convolution fusion | flops 537133056 | bytes 3932160 | tf_op jit(solution)/shard_map/dot_general | solution.py:23
  10.3 10.5 %collective-permute-start.11 = (bf16[256,512]{1,0:T(8,128)(2,1)S(1)}, bf16[256,512]{1,0:T(8,128)(2,1)S(1)}, u32[]{:S(2)}, u32[]{:S(2)}) collective-permute-start(bf16[256,512]{1,0:T(8,128)(2,1)S(1)} %fusion.44), channel_id=1, source_target_pairs={{1,2},{3,4},{5,6},{7,8},{9,10},{11,12},{13,14},{16,17},{18,19},{20... | collective-permute-start | bytes 786440 | tf_op jit(solution)/shard_map/ppermute | solution.py:19
  22.2 2.0 %fusion.22 = f32[256,1024]{1,0:T(8,128)S(1)} fusion(bf16[2048,2048]{1,0:T(8,128)(2,1)S(1)} %bitcast.18, f32[256,2048]{1,0:T(8,128)} %bitcast.35, bf16[256,2048]{1,0:T(8,128)(2,1)S(1)} %bitcast.39), kind=kOutput, calls=%fused_computation.20 | convolution fusion | flops 537133056 | bytes 4718592 | tf_op jit(solution)/shard_map/dot_general | solution.py:23
  24.1 2.8 %collective-permute-done.11 = bf16[256,512]{1,0:T(8,128)(2,1)S(1)} collective-permute-done((bf16[256,512]{1,0:T(8,128)(2,1)S(1)}, bf16[256,512]{1,0:T(8,128)(2,1)S(1)}, u32[]{:S(2)}, u32[]{:S(2)}) %collective-permute-start.11) | collective-permute-done | bytes 262176 | tf_op jit(solution)/shard_map/ppermute | solution.py:19
  31.2 2.9 %collective-permute-start.2 = (bf16[256,512]{1,0:T(8,128)(2,1)S(1)}, bf16[256,512]{1,0:T(8,128)(2,1)S(1)}, u32[]{:S(2)}, u32[]{:S(2)}) collective-permute-start(bf16[256,512]{1,0:T(8,128)(2,1)S(1)} %get-tuple-element.27), channel_id=1, source_target_pairs={{1,17},{3,19},{5,21},{7,23},{9,25},{11,27},{13,29},{15,31},{16,32}... | collective-permute-start | bytes 786440 | tf_op jit(solution)/shard_map/ppermute | solution.py:19
  34.0 8.9 %collective-permute-start.3 = (bf16[256,512]{1,0:T(8,128)(2,1)S(1)}, bf16[256,512]{1,0:T(8,128)(2,1)S(1)}, u32[]{:S(2)}, u32[]{:S(2)}) collective-permute-start(bf16[256,512]{1,0:T(8,128)(2,1)S(1)} %get-tuple-element.28), channel_id=1, source_target_pairs={{1,2},{3,4},{5,6},{7,8},{9,10},{11,12},{13,14},{16,17},{18,19},{20... | collective-permute-start | bytes 786440 | tf_op jit(solution)/shard_map/ppermute | solution.py:19
  43.7 1.3 collective-permute-start.14
  45.0 1.3 collective-permute-start.15
  46.3 3.7 %collective-permute-done.3 = bf16[256,512]{1,0:T(8,128)(2,1)S(1)} collective-permute-done((bf16[256,512]{1,0:T(8,128)(2,1)S(1)}, bf16[256,512]{1,0:T(8,128)(2,1)S(1)}, u32[]{:S(2)}, u32[]{:S(2)}) %collective-permute-start.3) | collective-permute-done | bytes 262176 | tf_op jit(solution)/shard_map/ppermute | solution.py:19
  56.8 3.2 %collective-permute-done.4 = bf16[256,512]{1,0:T(8,128)(2,1)S(1)} collective-permute-done((bf16[256,512]{1,0:T(8,128)(2,1)S(1)}, bf16[256,512]{1,0:T(8,128)(2,1)S(1)}, u32[]{:S(2)}, u32[]{:S(2)}) %collective-permute-start.4) | collective-permute-done | bytes 262176 | tf_op jit(solution)/shard_map/ppermute | solution.py:19
  60.8 7.2 %collective-permute-start.7 = (bf16[256,512]{1,0:T(8,128)(2,1)S(1)}, bf16[256,512]{1,0:T(8,128)(2,1)S(1)}, u32[]{:S(2)}, u32[]{:S(2)}) collective-permute-start(bf16[256,512]{1,0:T(8,128)(2,1)S(1)} %get-tuple-element.23), channel_id=1, source_target_pairs={{1,2},{3,4},{5,6},{7,8},{9,10},{11,12},{13,14},{16,17},{18,19},{20... | collective-permute-start | bytes 786440 | tf_op jit(solution)/shard_map/ppermute | solution.py:19
  68.0 1.4 %collective-permute-start.6 = (bf16[256,512]{1,0:T(8,128)(2,1)S(1)}, bf16[256,512]{1,0:T(8,128)(2,1)S(1)}, u32[]{:S(2)}, u32[]{:S(2)}) collective-permute-start(bf16[256,512]{1,0:T(8,128)(2,1)S(1)} %get-tuple-element.24), channel_id=1, source_target_pairs={{1,17},{3,19},{5,21},{7,23},{9,25},{11,27},{13,29},{15,31},{16,32}... | collective-permute-start | bytes 786440 | tf_op jit(solution)/shard_map/ppermute | solution.py:19
  70.2 2.6 %collective-permute-done.6 = bf16[256,512]{1,0:T(8,128)(2,1)S(1)} collective-permute-done((bf16[256,512]{1,0:T(8,128)(2,1)S(1)}, bf16[256,512]{1,0:T(8,128)(2,1)S(1)}, u32[]{:S(2)}, u32[]{:S(2)}) %collective-permute-start.6) | collective-permute-done | bytes 262176 | tf_op jit(solution)/shard_map/ppermute | solution.py:19
  73.7 1.3 collective-permute-start.21
  75.0 1.3 collective-permute-start.22
  84.2 9.3 %collective-permute-done.9 = bf16[256,512]{1,0:T(8,128)(2,1)S(1)} collective-permute-done((bf16[256,512]{1,0:T(8,128)(2,1)S(1)}, bf16[256,512]{1,0:T(8,128)(2,1)S(1)}, u32[]{:S(2)}, u32[]{:S(2)}) %collective-permute-start.9) | collective-permute-done | bytes 262176 | tf_op jit(solution)/shard_map/ppermute | solution.py:19
  95.5 1.3 collective-permute-start.19
  96.9 11.1 %collective-permute-done.24 = bf16[256,512]{1,0:T(8,128)(2,1)S(1)} collective-permute-done((bf16[256,512]{1,0:T(8,128)(2,1)S(1)}, bf16[256,512]{1,0:T(8,128)(2,1)S(1)}, u32[]{:S(2)}, u32[]{:S(2)}) %collective-permute-start.24) | collective-permute-done | bytes 262176 | tf_op jit(solution)/shard_map/ppermute | solution.py:19
  112.9 1.3 collective-permute-start.25
  115.6 2.5 %collective-permute-done.26 = bf16[256,512]{1,0:T(8,128)(2,1)S(1)} collective-permute-done((bf16[256,512]{1,0:T(8,128)(2,1)S(1)}, bf16[256,512]{1,0:T(8,128)(2,1)S(1)}, u32[]{:S(2)}, u32[]{:S(2)}) %collective-permute-start.26) | collective-permute-done | bytes 262176 | tf_op jit(solution)/shard_map/ppermute | solution.py:19
  118.8 11.9 %collective-permute-done.20 = bf16[256,512]{1,0:T(8,128)(2,1)S(1)} collective-permute-done((bf16[256,512]{1,0:T(8,128)(2,1)S(1)}, bf16[256,512]{1,0:T(8,128)(2,1)S(1)}, u32[]{:S(2)}, u32[]{:S(2)}) %collective-permute-start.20) | collective-permute-done | bytes 262176 | tf_op jit(solution)/shard_map/ppermute | solution.py:19
  130.6 1.7 %fusion.1 = bf16[1,1,256,2048]{3,2,1,0:T(8,128)(2,1)} fusion(f32[256,2048]{1,0:T(8,128)S(1)} %convolution_add_fusion, bf16[1,1,2048,2048]{3,2,1,0:T(8,128)(2,1)S(1)} %copy-done, bf16[256,512]{1,0:T(8,128)(2,1)S(1)} %collective-permute-done.20, bf16[256,512]{1,0:T(8,128)(2,1)S(1)} %collective-permute-done.25), kind=kOutput, calls=%fused_computation.3 | convolution fusion | flops 538050560 | bytes 5767168 | tf_op jit(solution)/shard_map/dot_general | solution.py:23
  (71 shorter events, 33.3 us)
Async XLA Ops:
  2.9 21.3 %collective-permute-start.10 = (bf16[256,512]{1,0:T(8,128)(2,1)S(1)}, bf16[256,512]{1,0:T(8,128)(2,1)S(1)}, u32[]{:S(2)}, u32[]{:S(2)}) collective-permute-start(bf16[256,512]{1,0:T(8,128)(2,1)S(1)} %fusion.47), channel_id=1, source_target_pairs={{1,17},{3,19},{5,21},{7,23},{9,25},{11,27},{13,29},{15,31},{16,32}... | collective-permute-start | bytes 786440 | tf_op jit(solution)/shard_map/ppermute | solution.py:19
  6.3 24.1 %collective-permute-start = (bf16[256,512]{1,0:T(8,128)(2,1)S(1)}, bf16[256,512]{1,0:T(8,128)(2,1)S(1)}, u32[]{:S(2)}, u32[]{:S(2)}) collective-permute-start(bf16[256,512]{1,0:T(8,128)(2,1)S(1)} %fusion.47), channel_id=1, source_target_pairs={{0,16},{2,18},{4,20},{6,22},{8,24},{10,26},{12,28},{14,30},{17,33}... | collective-permute-start | bytes 786440 | tf_op jit(solution)/shard_map/ppermute | solution.py:19
  10.3 16.6 %collective-permute-start.11 = (bf16[256,512]{1,0:T(8,128)(2,1)S(1)}, bf16[256,512]{1,0:T(8,128)(2,1)S(1)}, u32[]{:S(2)}, u32[]{:S(2)}) collective-permute-start(bf16[256,512]{1,0:T(8,128)(2,1)S(1)} %fusion.44), channel_id=1, source_target_pairs={{1,2},{3,4},{5,6},{7,8},{9,10},{11,12},{13,14},{16,17},{18,19},{20... | collective-permute-start | bytes 786440 | tf_op jit(solution)/shard_map/ppermute | solution.py:19
  20.9 9.5 %collective-permute-start.1 = (bf16[256,512]{1,0:T(8,128)(2,1)S(1)}, bf16[256,512]{1,0:T(8,128)(2,1)S(1)}, u32[]{:S(2)}, u32[]{:S(2)}) collective-permute-start(bf16[256,512]{1,0:T(8,128)(2,1)S(1)} %fusion.44), channel_id=1, source_target_pairs={{0,1},{2,3},{4,5},{6,7},{8,9},{10,11},{12,13},{14,15},{17,18},{19,... | collective-permute-start | bytes 786440 | tf_op jit(solution)/shard_map/ppermute | solution.py:19
  27.7 15.2 %collective-permute-start.12 = (bf16[256,512]{1,0:T(8,128)(2,1)S(1)}, bf16[256,512]{1,0:T(8,128)(2,1)S(1)}, u32[]{:S(2)}, u32[]{:S(2)}) collective-permute-start(bf16[256,512]{1,0:T(8,128)(2,1)S(1)} %get-tuple-element.21), channel_id=1, source_target_pairs={{0,16},{2,18},{4,20},{6,22},{8,24},{10,26},{12,28},{14,30},{17,33}... | collective-permute-start | bytes 786440 | tf_op jit(solution)/shard_map/ppermute | solution.py:19
  29.0 13.9 %collective-permute-start.13 = (bf16[256,512]{1,0:T(8,128)(2,1)S(1)}, bf16[256,512]{1,0:T(8,128)(2,1)S(1)}, u32[]{:S(2)}, u32[]{:S(2)}) collective-permute-start(bf16[256,512]{1,0:T(8,128)(2,1)S(1)} %get-tuple-element.22), channel_id=1, source_target_pairs={{0,1},{2,3},{4,5},{6,7},{8,9},{10,11},{12,13},{14,15},{17,18},{19,... | collective-permute-start | bytes 786440 | tf_op jit(solution)/shard_map/ppermute | solution.py:19
  31.2 15.2 %collective-permute-start.2 = (bf16[256,512]{1,0:T(8,128)(2,1)S(1)}, bf16[256,512]{1,0:T(8,128)(2,1)S(1)}, u32[]{:S(2)}, u32[]{:S(2)}) collective-permute-start(bf16[256,512]{1,0:T(8,128)(2,1)S(1)} %get-tuple-element.27), channel_id=1, source_target_pairs={{1,17},{3,19},{5,21},{7,23},{9,25},{11,27},{13,29},{15,31},{16,32}... | collective-permute-start | bytes 786440 | tf_op jit(solution)/shard_map/ppermute | solution.py:19
  34.0 16.0 %collective-permute-start.3 = (bf16[256,512]{1,0:T(8,128)(2,1)S(1)}, bf16[256,512]{1,0:T(8,128)(2,1)S(1)}, u32[]{:S(2)}, u32[]{:S(2)}) collective-permute-start(bf16[256,512]{1,0:T(8,128)(2,1)S(1)} %get-tuple-element.28), channel_id=1, source_target_pairs={{1,2},{3,4},{5,6},{7,8},{9,10},{11,12},{13,14},{16,17},{18,19},{20... | collective-permute-start | bytes 786440 | tf_op jit(solution)/shard_map/ppermute | solution.py:19
  43.7 9.7 %collective-permute-start.14 = (bf16[256,512]{1,0:T(8,128)(2,1)S(1)}, bf16[256,512]{1,0:T(8,128)(2,1)S(1)}, u32[]{:S(2)}, u32[]{:S(2)}) collective-permute-start(bf16[256,512]{1,0:T(8,128)(2,1)S(1)} %get-tuple-element.19), channel_id=1, source_target_pairs={{1,17},{3,19},{5,21},{7,23},{9,25},{11,27},{13,29},{15,31},{16,32}... | collective-permute-start | bytes 786440 | tf_op jit(solution)/shard_map/ppermute | solution.py:19
  45.0 8.4 %collective-permute-start.15 = (bf16[256,512]{1,0:T(8,128)(2,1)S(1)}, bf16[256,512]{1,0:T(8,128)(2,1)S(1)}, u32[]{:S(2)}, u32[]{:S(2)}) collective-permute-start(bf16[256,512]{1,0:T(8,128)(2,1)S(1)} %get-tuple-element.20), channel_id=1, source_target_pairs={{1,2},{3,4},{5,6},{7,8},{9,10},{11,12},{13,14},{16,17},{18,19},{20... | collective-permute-start | bytes 786440 | tf_op jit(solution)/shard_map/ppermute | solution.py:19
  50.8 9.2 %collective-permute-start.4 = (bf16[256,512]{1,0:T(8,128)(2,1)S(1)}, bf16[256,512]{1,0:T(8,128)(2,1)S(1)}, u32[]{:S(2)}, u32[]{:S(2)}) collective-permute-start(bf16[256,512]{1,0:T(8,128)(2,1)S(1)} %get-tuple-element.25), channel_id=1, source_target_pairs={{0,16},{2,18},{4,20},{6,22},{8,24},{10,26},{12,28},{14,30},{17,33}... | collective-permute-start | bytes 786440 | tf_op jit(solution)/shard_map/ppermute | solution.py:19
  52.1 7.9 %collective-permute-start.5 = (bf16[256,512]{1,0:T(8,128)(2,1)S(1)}, bf16[256,512]{1,0:T(8,128)(2,1)S(1)}, u32[]{:S(2)}, u32[]{:S(2)}) collective-permute-start(bf16[256,512]{1,0:T(8,128)(2,1)S(1)} %get-tuple-element.26), channel_id=1, source_target_pairs={{0,1},{2,3},{4,5},{6,7},{8,9},{10,11},{12,13},{14,15},{17,18},{19,... | collective-permute-start | bytes 786440 | tf_op jit(solution)/shard_map/ppermute | solution.py:19
  54.1 18.7 %collective-permute-start.16 = (bf16[256,512]{1,0:T(8,128)(2,1)S(1)}, bf16[256,512]{1,0:T(8,128)(2,1)S(1)}, u32[]{:S(2)}, u32[]{:S(2)}) collective-permute-start(bf16[256,512]{1,0:T(8,128)(2,1)S(1)} %get-tuple-element.17), channel_id=1, source_target_pairs={{0,16},{2,18},{4,20},{6,22},{8,24},{10,26},{12,28},{14,30},{17,33}... | collective-permute-start | bytes 786440 | tf_op jit(solution)/shard_map/ppermute | solution.py:19
  55.5 17.4 %collective-permute-start.17 = (bf16[256,512]{1,0:T(8,128)(2,1)S(1)}, bf16[256,512]{1,0:T(8,128)(2,1)S(1)}, u32[]{:S(2)}, u32[]{:S(2)}) collective-permute-start(bf16[256,512]{1,0:T(8,128)(2,1)S(1)} %get-tuple-element.18), channel_id=1, source_target_pairs={{0,1},{2,3},{4,5},{6,7},{8,9},{10,11},{12,13},{14,15},{17,18},{19,... | collective-permute-start | bytes 786440 | tf_op jit(solution)/shard_map/ppermute | solution.py:19
  60.8 12.0 %collective-permute-start.7 = (bf16[256,512]{1,0:T(8,128)(2,1)S(1)}, bf16[256,512]{1,0:T(8,128)(2,1)S(1)}, u32[]{:S(2)}, u32[]{:S(2)}) collective-permute-start(bf16[256,512]{1,0:T(8,128)(2,1)S(1)} %get-tuple-element.23), channel_id=1, source_target_pairs={{1,2},{3,4},{5,6},{7,8},{9,10},{11,12},{13,14},{16,17},{18,19},{20... | collective-permute-start | bytes 786440 | tf_op jit(solution)/shard_map/ppermute | solution.py:19
  77.1 7.1 %collective-permute-start.8 = (bf16[256,512]{1,0:T(8,128)(2,1)S(1)}, bf16[256,512]{1,0:T(8,128)(2,1)S(1)}, u32[]{:S(2)}, u32[]{:S(2)}) collective-permute-start(bf16[256,512]{1,0:T(8,128)(2,1)S(1)} %get-tuple-element.15), channel_id=1, source_target_pairs={{17,1},{19,3},{21,5},{23,7},{25,9},{27,11},{29,13},{31,15},{32,16}... | collective-permute-start | bytes 786440 | tf_op jit(solution)/shard_map/ppermute | solution.py:19
  78.4 15.1 %collective-permute-start.9 = (bf16[256,512]{1,0:T(8,128)(2,1)S(1)}, bf16[256,512]{1,0:T(8,128)(2,1)S(1)}, u32[]{:S(2)}, u32[]{:S(2)}) collective-permute-start(bf16[256,512]{1,0:T(8,128)(2,1)S(1)} %get-tuple-element.16), channel_id=1, source_target_pairs={{2,1},{4,3},{6,5},{8,7},{10,9},{12,11},{14,13},{17,16},{19,18},{21... | collective-permute-start | bytes 786440 | tf_op jit(solution)/shard_map/ppermute | solution.py:19
  80.5 16.4 %collective-permute-start.23 = (bf16[256,512]{1,0:T(8,128)(2,1)S(1)}, bf16[256,512]{1,0:T(8,128)(2,1)S(1)}, u32[]{:S(2)}, u32[]{:S(2)}) collective-permute-start(bf16[256,512]{1,0:T(8,128)(2,1)S(1)} %get-tuple-element.9), channel_id=1, source_target_pairs={{17,1},{19,3},{21,5},{23,7},{25,9},{27,11},{29,13},{31,15},{32,16}... | collective-permute-start | bytes 786440 | tf_op jit(solution)/shard_map/ppermute | solution.py:19
  81.8 26.2 %collective-permute-start.24 = (bf16[256,512]{1,0:T(8,128)(2,1)S(1)}, bf16[256,512]{1,0:T(8,128)(2,1)S(1)}, u32[]{:S(2)}, u32[]{:S(2)}) collective-permute-start(bf16[256,512]{1,0:T(8,128)(2,1)S(1)} %get-tuple-element.10), channel_id=1, source_target_pairs={{2,1},{4,3},{6,5},{8,7},{10,9},{12,11},{14,13},{17,16},{19,18},{21... | collective-permute-start | bytes 786440 | tf_op jit(solution)/shard_map/ppermute | solution.py:19
  94.2 15.9 %collective-permute-start.18 = (bf16[256,512]{1,0:T(8,128)(2,1)S(1)}, bf16[256,512]{1,0:T(8,128)(2,1)S(1)}, u32[]{:S(2)}, u32[]{:S(2)}) collective-permute-start(bf16[256,512]{1,0:T(8,128)(2,1)S(1)} %get-tuple-element.13), channel_id=1, source_target_pairs={{16,0},{18,2},{20,4},{22,6},{24,8},{26,10},{28,12},{30,14},{33,17}... | collective-permute-start | bytes 786440 | tf_op jit(solution)/shard_map/ppermute | solution.py:19
  95.5 14.6 %collective-permute-start.19 = (bf16[256,512]{1,0:T(8,128)(2,1)S(1)}, bf16[256,512]{1,0:T(8,128)(2,1)S(1)}, u32[]{:S(2)}, u32[]{:S(2)}) collective-permute-start(bf16[256,512]{1,0:T(8,128)(2,1)S(1)} %get-tuple-element.14), channel_id=1, source_target_pairs={{1,0},{3,2},{5,4},{7,6},{9,8},{11,10},{13,12},{15,14},{18,17},{20,... | collective-permute-start | bytes 786440 | tf_op jit(solution)/shard_map/ppermute | solution.py:19
  108.8 6.7 %collective-permute-start.27 = (bf16[256,512]{1,0:T(8,128)(2,1)S(1)}, bf16[256,512]{1,0:T(8,128)(2,1)S(1)}, u32[]{:S(2)}, u32[]{:S(2)}) collective-permute-start(bf16[256,512]{1,0:T(8,128)(2,1)S(1)} %get-tuple-element.6), channel_id=1, source_target_pairs={{16,0},{18,2},{20,4},{22,6},{24,8},{26,10},{28,12},{30,14},{33,17}... | collective-permute-start | bytes 786440 | tf_op jit(solution)/shard_map/ppermute | solution.py:19
  110.9 7.1 %collective-permute-start.26 = (bf16[256,512]{1,0:T(8,128)(2,1)S(1)}, bf16[256,512]{1,0:T(8,128)(2,1)S(1)}, u32[]{:S(2)}, u32[]{:S(2)}) collective-permute-start(bf16[256,512]{1,0:T(8,128)(2,1)S(1)} %get-tuple-element.8), channel_id=1, source_target_pairs={{17,1},{19,3},{21,5},{23,7},{25,9},{27,11},{29,13},{31,15},{32,16}... | collective-permute-start | bytes 786440 | tf_op jit(solution)/shard_map/ppermute | solution.py:19
  114.3 16.4 %collective-permute-start.20 = (bf16[256,512]{1,0:T(8,128)(2,1)S(1)}, bf16[256,512]{1,0:T(8,128)(2,1)S(1)}, u32[]{:S(2)}, u32[]{:S(2)}) collective-permute-start(bf16[256,512]{1,0:T(8,128)(2,1)S(1)} %get-tuple-element.7), channel_id=1, source_target_pairs={{2,1},{4,3},{6,5},{8,7},{10,9},{12,11},{14,13},{17,16},{19,18},{21... | collective-permute-start | bytes 786440 | tf_op jit(solution)/shard_map/ppermute | solution.py:19
  (7 other events, 67.6 us)
